TPU v7x, 128 devices: a whole 4x4x4 slice. The times are simulated.
128 devices in a mesh: batch: 8 (over y_lo, x), corpus: 16 (over z, y_hi, core).
Axes of the slice: x: 4, y: 4 (y_hi: 2, y_lo: 2; y = y_hi * 2 + y_lo), z: 4, core: 2. Of those that a mesh axis runs over, the one named last changes fastest.
Arguments:
- states: bfloat16 [8192, 4096], P('batch', 'corpus'), may hold values from -6 to 6
- norm_gain: float32 [4096], replicated, may hold values from 0.25 to 1.75
- gate_weight: bfloat16 [4096, 12288], P('batch', 'corpus'), may hold values from -0.09375 to 0.09375
- up_weight: bfloat16 [4096, 12288], P('batch', 'corpus'), may hold values from -0.09375 to 0.09375
- down_weight: bfloat16 [12288, 4096], P('corpus', 'batch'), may hold values from -0.0546875 to 0.0546875
- final_gain: float32 [4096], replicated, may hold values from 0.25 to 1.75
- hash_weight: bfloat16 [4096, 1024], replicated, may hold values from -0.75 to 0.75
- query_bits: bfloat16 [4096, 1024], replicated, may hold values from -1 to 1
- slot_map: int32 [128], replicated, may hold values from 0 to 127, each once
- query_index: int32 [4096, 100], replicated, may hold values from 0 to 127
Outputs:
- scores: float32 [4096, 100], P(('batch', 'corpus'))
Inputs may be any that keep to these rules, and one draw needn't show every extreme that they name: `slot_map`: each corpus entry is named by exactly one document.
All inputs are finite; a program needn't handle non-finite values.
Results may differ from a plain program's by a relative error of at most 0.017.
Values may be sent and summed in bfloat16 or wider, within the bound.
No kernel may reach another device: no remote copies, remote signals or barrier semaphores. Data moves between devices by JAX's collectives and lax.ppermute only.
A program may use at most 192 MiB of HBM per device.

v0:
```python
import jax
import jax.numpy as jnp
from jax import lax
from jax.sharding import PartitionSpec as P

DOC_LEN = 64
CODE = 1024
NQ = 4096


def side_by_side(arrays, axis, dim, along):
    both = jnp.concatenate(arrays, axis=along)
    whole, at, gathered = (lax.all_gather(both, axis, axis=dim, tiled=True), 0, [])
    for a in arrays:
        gathered.append(lax.slice_in_dim(whole, at, at + a.shape[along], axis=along))
        at += a.shape[along]
    return tuple(gathered)


def rms(values, gain):
    return values * lax.rsqrt(jnp.mean(values * values, axis=-1, keepdims=True) + 1e-06) * gain


def add_rows(left, piece):
    return jnp.dot(left, piece, preferred_element_type=jnp.float32)


def local(
    states,
    norm_gain,
    gate_weight,
    up_weight,
    down_weight,
    final_gain,
    hash_weight,
    query_bits,
    slot_map,
    query_index,
):
    corpus_count = lax.axis_size("corpus")
    devices = lax.axis_size("batch") * corpus_count
    flat_index = lax.axis_index("batch") * corpus_count + lax.axis_index("corpus")
    whole = lax.all_gather(states, "corpus", axis=1, tiled=True)
    normed = rms(whole.astype(jnp.float32), norm_gain).astype(jnp.bfloat16)
    pieces = side_by_side((gate_weight, up_weight), "batch", 0, 1)
    gate = add_rows(normed, pieces[0])
    up = add_rows(normed, pieces[1])
    hidden = (jax.nn.silu(gate) * up).astype(jnp.bfloat16)
    terms = jnp.dot(
        hidden,
        lax.all_gather(down_weight, "batch", axis=1, tiled=True),
        preferred_element_type=jnp.float32,
    )
    ffn = lax.psum_scatter(
        terms.astype(jnp.bfloat16), "corpus", scatter_dimension=0, tiled=True
    ).astype(jnp.float32)
    own_rows = ffn.shape[0]
    mine = lax.dynamic_slice_in_dim(whole, lax.axis_index("corpus") * own_rows, own_rows, 0)
    resid = mine.astype(jnp.float32) + ffn
    finals = rms(resid, final_gain)
    owned_docs = own_rows // DOC_LEN
    pooled = jnp.mean(finals.reshape(owned_docs, DOC_LEN, finals.shape[1]), axis=1).astype(
        jnp.bfloat16
    )
    codes = jnp.tanh(jnp.dot(pooled, hash_weight, preferred_element_type=jnp.float32)).astype(
        jnp.bfloat16
    )
    doc_total = owned_docs * devices
    scale = 1.0 / jnp.sqrt(jnp.float32(CODE))
    gathered = lax.all_gather(codes, ("batch", "corpus"), axis=0, tiled=True)
    placing = (slot_map[:, None] == jnp.arange(doc_total, dtype=jnp.int32)[None, :]).astype(
        jnp.bfloat16
    )
    corpus = jnp.einsum("ds,dc->sc", placing, gathered, preferred_element_type=jnp.float32).astype(
        jnp.bfloat16
    )
    query_rows = NQ // devices
    my_bits = lax.dynamic_slice_in_dim(query_bits, flat_index * query_rows, query_rows, 0)
    my_index = lax.dynamic_slice_in_dim(query_index, flat_index * query_rows, query_rows, 0)
    table = jnp.dot(my_bits, corpus.T, preferred_element_type=jnp.float32) * scale
    scores = jnp.take_along_axis(table, my_index, axis=1)
    return scores


def solution(mesh):
    placed = (
        P("batch", "corpus"),
        P(),
        P("batch", "corpus"),
        P("batch", "corpus"),
        P("corpus", "batch"),
        P(),
        P(),
        P(),
        P(),
        P(),
    )
    return jax.shard_map(
        local, mesh=mesh, in_specs=placed, out_specs=P(("batch", "corpus"), None), check_vma=False
    )
```

profile of v0, /device:TPU:1, one launch (start us, length us, event | category | flops | bytes accessed | tf_op | source)
XLA Modules:
  0.0 631.7 jit_solution(1051141560968313369)
XLA Ops:
  6.5 0.0 copy-start
  6.5 0.0 all-gather.5.cloned.1.call-start
  6.5 0.7 all-gather.5.cloned.1.call-update
  7.3 0.0 copy-start.3
  7.3 0.0 all-gather.7.cloned.1.call-start
  7.3 2.7 pad_maximum_fusion
  10.0 0.0 all-gather.7.cloned.1.call-update
  10.0 0.0 all-gather.9.cloned.1.call-start
  10.1 0.7 all-gather.9.cloned.1.call-update
  10.7 0.0 reduce-scatter.2.cloned.1.call-start
  10.8 79.1 %all-gather.5.cloned.1.call-done = bf16[1024,4096]{1,0:T(8,128)(2,1)} async-done(((bf16[1024,256]{1,0:T(8,128)(2,1)}), bf16[1024,4096]{1,0:T(8,128)(2,1)}) %all-gather.5.cloned.1.call-update) | async-done | bytes 8388624 | tf_op jit(solution)/shard_map/all_gather | solution.py:43
  89.9 5.1 fusion
  95.0 124.5 %all-gather.7.cloned.1.call-done = bf16[4096,1536]{1,0:T(8,128)(2,1)} async-done(((bf16[512,1536]{1,0:T(8,128)(2,1)}), bf16[4096,1536]{1,0:T(8,128)(2,1)}) %all-gather.7.cloned.1.call-update) | async-done | bytes 12582928 | tf_op jit(solution)/shard_map/all_gather | solution.py:13
  219.5 0.0 copy-done.3
  219.5 12.4 %fusion.3 = f32[1024,768]{1,0:T(8,128)} fusion(bf16[4096,1536]{1,0:T(8,128)(2,1)} %all-gather.7.cloned.1.call-done, bf16[1024,4096]{1,0:T(8,128)(2,1)} %all-gather.5.cloned.1.call-done, f32[4096]{0:T(1024)S(1)} %copy-done.3, f32[1024]{0:T(1024)S(1)} %add_rsqrt_fusion), kind=kOutput, calls=%fused_computation.7 | convolution fusion | flops 6459228160 | bytes 17846272 | tf_op jit(solution)/shard_map/dot_general | solution.py:25
  231.9 60.2 %all-gather.9.cloned.1.call-done = bf16[768,4096]{1,0:T(8,128)(2,1)} async-done(((bf16[768,512]{1,0:T(8,128)(2,1)}), bf16[768,4096]{1,0:T(8,128)(2,1)}) %all-gather.9.cloned.1.call-update) | async-done | bytes 6291472 | tf_op jit(solution)/shard_map/all_gather | solution.py:51
  292.1 26.3 %convolution_convert_fusion = bf16[1024,4096]{1,0:T(8,128)(2,1)} fusion(bf16[768,4096]{1,0:T(8,128)(2,1)} %all-gather.9.cloned.1.call-done, f32[1024,768]{1,0:T(8,128)} %fusion.3, bf16[4096,1536]{1,0:T(8,128)(2,1)} %all-gather.7.cloned.1.call-done, bf16[1024,4096]{1,0:T(8,128)(2,1)} %all-gather.5.cloned.1.call-done, f32[4096]{0:T(1024)S(1)} %copy-done.3, ...), kind=kOutput, calls=%fused_computation.6 | convolution fusion | flops 12910592000 | bytes 32526336 | tf_op jit(solution)/shard_map/dot_general | solution.py:49
  318.4 0.0 copy-start.1
  318.4 0.0 reduce-scatter.2.cloned.1.call-update
  318.4 0.0 copy-done
  318.4 0.1 constant_dynamic-slice_fusion
  318.5 0.1 copy.14
  318.6 0.1 reshape.40
  318.7 99.8 %reduce-scatter.2.cloned.1.call-done = bf16[64,4096]{1,0:T(8,128)(2,1)} async-done(((bf16[1024,4096]{1,0:T(8,128)(2,1)}), bf16[64,4096]{1,0:T(8,128)(2,1)}) %reduce-scatter.2.cloned.1.call-update) | async-done | bytes 524304 | tf_op jit(solution)/shard_map/reduce_scatter | solution.py:54
  418.5 1.5 multiply_reduce_fusion.1
  420.0 0.0 copy-done.1
  420.0 1.5 multiply_reduce_fusion
  421.5 0.0 copy-start.2
  421.5 4.6 fusion.25
  426.1 177.8 %all-gather = bf16[131072]{0:T(1024)(128)(2,1)S(1)} all-gather(bf16[1024]{0:T(1024)(128)(2,1)S(1)} %tanh_convert_fusion), channel_id=2, replica_groups=mesh['batch'=8,'corpus'=16] {'batch','corpus'}, dimensions={0}, use_global_device_ids=true | all-gather | bytes 264192 | tf_op jit(solution)/shard_map/all_gather | solution.py:70
  603.9 0.1 reshape.46
  604.1 0.0 copy-done.2
  604.1 1.3 fusion.19
  605.4 19.0 %gather_fusion = f32[3200]{0:T(1024)S(1)} fusion(f32[32,128]{1,0:T(8,128)S(1)} %fusion.19, s32[3200]{0:T(1024)S(1)} %reshape.40), kind=kCustom, calls=%fused_computation | custom fusion | bytes 51200 | tf_op jit(solution)/shard_map/jit(take_along_axis)/gather | solution.py:81
  624.4 0.1 reshape.43
  624.5 0.6 and_select_fusion
  (6 shorter events, 0.1 us)
Async XLA Ops:
  6.5 311.9 %copy-start = (s32[4096,100]{0,1:T(8,128)S(1)}, s32[4096,100]{0,1:T(8,128)}, u32[]{:S(2)}) copy-start(s32[4096,100]{0,1:T(8,128)} %param.19) | copy-start | bytes 4915204
  6.5 83.3 %all-gather.5.cloned.1.call-start = ((), (), s32[]{:S(2)}) async-start(), calls=%async_computation.1 | async-start | bytes 8912896 | tf_op jit(solution)/shard_map/all_gather | solution.py:43
  7.3 212.2 %copy-start.3 = (f32[4096]{0:T(1024)S(1)}, f32[4096]{0:T(1024)}, u32[]{:S(2)}) copy-start(f32[4096]{0:T(1024)} %param.11) | copy-start | bytes 49156
  7.3 212.2 %all-gather.7.cloned.1.call-start = ((), (), s32[]{:S(2)}) async-start(), calls=%async_computation.2 | async-start | bytes 14155776 | tf_op jit(solution)/shard_map/all_gather | solution.py:13
  10.0 282.1 %all-gather.9.cloned.1.call-start = ((), (), s32[]{:S(2)}) async-start(), calls=%async_computation.3 | async-start | bytes 7077888 | tf_op jit(solution)/shard_map/all_gather | solution.py:51
  10.7 407.8 %reduce-scatter.2.cloned.1.call-start = ((), (), s32[]{:S(2)}) async-start(), calls=%async_computation.4 | async-start | bytes 8912896 | tf_op jit(solution)/shard_map/reduce_scatter | solution.py:54
  318.4 101.6 %copy-start.1 = (f32[4096]{0:T(1024)S(1)}, f32[4096]{0:T(1024)}, u32[]{:S(2)}) copy-start(f32[4096]{0:T(1024)} %param.15) | copy-start | bytes 49156
  421.5 182.6 %copy-start.2 = (s32[128]{0:T(128)S(1)}, s32[128]{0:T(128)}, u32[]{:S(2)}) copy-start(s32[128]{0:T(128)} %param.18) | copy-start | bytes 1540
Sparse Core Ops, SparseCore 0:
  9.7 80.1 all-gather.4
  91.5 127.9 all-gather.6
  221.1 70.9 all-gather.8
  318.5 99.9 reduce-scatter.1
where the time goes:
time: 632 us
  waiting for transfers between devices  365 us (58%)
  blocking collectives  178 us (28%)
  matrix products  44.6 us (7%)
  local copies, waits for them, and re-layouts  19.5 us (3%)
  between operations  13.2 us (2%)
  other arithmetic  11.3 us (2%)
    all_gather x1, blocking collectives, local(): gathered = lax.all_gather(codes, ('batch', 'corpus'), axis=0, tiled=True)  178 us
    all_gather x1, waiting for transfers between devices, side_by_side(): lax.all_gather(both, axis, axis=dim, tiled=True)  125 us
    reduce_scatter x1, waiting for transfers between devices, local(): lax.psum_scatter(terms.astype(jnp.bfloat16), 'corpus', scatter_dimension=...  99.8 us
    all_gather x1, waiting for transfers between devices, local(): whole = lax.all_gather(states, 'corpus', axis=1, tiled=True)  79.1 us
    all_gather x1, waiting for transfers between devices, local(): lax.all_gather(down_weight, 'batch', axis=1, tiled=True)  60.2 us
    dot_general x1, matrix products, local(): jnp.dot(hidden, lax.all_gather(down_weight, 'batch', axis=1, tiled=True),...  26.3 us
    gather x3, local copies, waits for them, and re-layouts, local(): scores = jnp.take_along_axis(table, my_index, axis=1)  19.2 us
  transfers between devices with their start and end apart: 4, of which 4 were waited for; matrix products, arithmetic and copies ran while one was open for 3% of the time, Pallas kernels for 0%

commit v1 on v0

--- a/solution.py
+++ b/solution.py
@@ -40,7 +40,9 @@
     corpus_count = lax.axis_size("corpus")
     devices = lax.axis_size("batch") * corpus_count
     flat_index = lax.axis_index("batch") * corpus_count + lax.axis_index("corpus")
-    whole = lax.all_gather(states, "corpus", axis=1, tiled=True)
+    whole = jnp.concatenate(
+        lax.all_to_all(jnp.stack([states] * lax.axis_size("corpus")), "corpus", 0, 0), axis=1
+    )
     normed = rms(whole.astype(jnp.float32), norm_gain).astype(jnp.bfloat16)
     pieces = side_by_side((gate_weight, up_weight), "batch", 0, 1)
     gate = add_rows(normed, pieces[0])

time: 632 us -> 657 us (1.040)
  blocking collectives: 178 us -> 460 us
  waiting for transfers between devices: 365 us -> 98.3 us
  local copies, waits for them, and re-layouts: 19.5 us -> 29.1 us
    all_to_all x0 -> x1, blocking collectives: none -> 282 us  [local(): lax.all_to_all(jnp.stack([states] * lax.axis_size('corpus')), 'corpus', 0...]
    all_gather x1, waiting for transfers between devices: 125 us -> 0.02 us  [side_by_side(): lax.all_gather(both, axis, axis=dim, tiled=True)]
    all_gather x1 -> x0, waiting for transfers between devices: 79.1 us -> none  [local(): whole = lax.all_gather(states, 'corpus', axis=1, tiled=True)]
    all_gather x1, waiting for transfers between devices: 60.2 us -> 0.01 us  [local(): lax.all_gather(down_weight, 'batch', axis=1, tiled=True)]
    reshape x0 -> x1, local copies, waits for them, and re-layouts: none -> 7.75 us  [local(): jnp.concatenate(lax.all_to_all(jnp.stack([states] * lax.axis_size('corpus...]
  transfers between devices with their start and end apart: 4 -> 3, of which waited for: 4 -> 1; matrix products, arithmetic and copies ran while one was open for 3% -> 4% of each run, Pallas kernels for 0% -> 0%
where the time goes in v1:
time: 657 us; the launch traced here: 656 us
  blocking collectives  460 us (70%)
  waiting for transfers between devices  98.3 us (15%)
  matrix products  44.6 us (7%)
  local copies, waits for them, and re-layouts  29.1 us (4%)
  between operations  13.2 us (2%)
  other arithmetic  11.4 us (2%)
    all_to_all x1, blocking collectives, local(): lax.all_to_all(jnp.stack([states] * lax.axis_size('corpus')), 'corpus', 0...  282 us
    all_gather x1, blocking collectives, local(): gathered = lax.all_gather(codes, ('batch', 'corpus'), axis=0, tiled=True)  178 us
    reduce_scatter x1, waiting for transfers between devices, local(): lax.psum_scatter(terms.astype(jnp.bfloat16), 'corpus', scatter_dimension=...  97.5 us
    dot_general x1, matrix products, local(): jnp.dot(hidden, lax.all_gather(down_weight, 'batch', axis=1, tiled=True),...  26.3 us
    gather x3, local copies, waits for them, and re-layouts, local(): scores = jnp.take_along_axis(table, my_index, axis=1)  19.2 us
  transfers between devices with their start and end apart: 3, of which 1 were waited for; matrix products, arithmetic and copies ran while one was open for 4% of the time, Pallas kernels for 0%

profile of v1, /device:TPU:1, one launch (start us, length us, event | category | flops | bytes accessed | tf_op | source)
XLA Modules:
  0.0 656.3 jit_solution(8743944974505867459)
XLA Ops:
  6.5 0.0 copy-start
  6.5 0.0 all-gather.4.cloned.1.call-start
  6.5 2.7 pad_maximum_fusion
  9.3 0.0 all-gather.4.cloned.1.call-update
  9.3 0.0 all-gather.6.cloned.1.call-start
  9.4 0.7 all-gather.6.cloned.1.call-update
  10.1 0.0 reduce-scatter.2.cloned.1.call-start
  10.1 1.8 stack.2
  12.0 281.7 %all_to_all.5 = bf16[16,1024,256]{2,1,0:T(8,128)(2,1)} all-to-all(bf16[16,1024,256]{2,1,0:T(8,128)(2,1)S(1)} %stack.2), channel_id=1, replica_groups=mesh['batch'=8,'corpus'=16] {'corpus'}, dimensions={0} | all-to-all | bytes 16777216 | tf_op jit(solution)/shard_map/all_to_all | solution.py:44
  293.7 7.7 %copy.16 = bf16[16,128,8,256]{3,2,0,1:T(8,128)(2,1)} copy(bf16[16,128,8,256]{3,2,1,0:T(8,128)(2,1)} %bitcast.13) | data formatting | bytes 16777216 | tf_op jit(solution)/shard_map/reshape | solution.py:43
  301.4 0.0 copy-start.3
  301.4 5.1 multiply_reduce_fusion
  306.5 0.0 all-gather.4.cloned.1.call-done
  306.6 0.0 copy-done.3
  306.6 12.4 %fusion = f32[1024,768]{1,0:T(8,128)} fusion(bf16[4096,1536]{1,0:T(8,128)(2,1)} %all-gather.4.cloned.1.call-done, bf16[1024,4096]{1,0:T(8,128)(2,1)} %bitcast.14, f32[4096]{0:T(1024)S(1)} %copy-done.3, f32[1024]{0:T(1024)S(1)} %add_rsqrt_fusion), kind=kOutput, calls=%fused_computation.4 | convolution fusion | flops 6459228160 | bytes 17846272 | tf_op jit(solution)/shard_map/dot_general | solution.py:25
  319.0 0.0 all-gather.6.cloned.1.call-done
  319.0 26.3 %convolution_convert_fusion = bf16[1024,4096]{1,0:T(8,128)(2,1)} fusion(bf16[768,4096]{1,0:T(8,128)(2,1)} %all-gather.6.cloned.1.call-done, f32[1024,768]{1,0:T(8,128)} %fusion, bf16[4096,1536]{1,0:T(8,128)(2,1)} %all-gather.4.cloned.1.call-done, bf16[1024,4096]{1,0:T(8,128)(2,1)} %bitcast.15, f32[4096]{0:T(1024)S(1)} %copy-done.3, f32[1024]{0:T(1024)S(1)} %add_rsqrt_fusion), kind=kOutput, calls=%fused_computation.3 | convolution fusion | flops 12910592000 | bytes 32526336 | tf_op jit(solution)/shard_map/dot_general | solution.py:51
  345.3 0.0 copy-start.1
  345.3 0.0 reduce-scatter.2.cloned.1.call-update
  345.3 0.0 copy-done
  345.3 0.1 constant_dynamic-slice_fusion
  345.4 0.1 copy.15
  345.5 0.1 reshape.50
  345.6 97.5 %reduce-scatter.2.cloned.1.call-done = bf16[64,4096]{1,0:T(8,128)(2,1)} async-done(((bf16[1024,4096]{1,0:T(8,128)(2,1)}), bf16[64,4096]{1,0:T(8,128)(2,1)}) %reduce-scatter.2.cloned.1.call-update) | async-done | bytes 524304 | tf_op jit(solution)/shard_map/reduce_scatter | solution.py:56
  443.1 1.5 multiply_reduce_fusion.2
  444.6 0.0 copy-done.1
  444.6 1.5 multiply_reduce_fusion.1
  446.1 0.0 copy-start.2
  446.1 4.6 fusion.16
  450.7 177.8 %all-gather = bf16[131072]{0:T(1024)(128)(2,1)S(1)} all-gather(bf16[1024]{0:T(1024)(128)(2,1)S(1)} %tanh_convert_fusion), channel_id=2, replica_groups=mesh['batch'=8,'corpus'=16] {'batch','corpus'}, dimensions={0}, use_global_device_ids=true | all-gather | bytes 264192 | tf_op jit(solution)/shard_map/all_gather | solution.py:72
  628.5 0.1 reshape.56
  628.7 0.0 copy-done.2
  628.7 1.3 fusion.10
  630.0 19.0 %gather_fusion = f32[3200]{0:T(1024)S(1)} fusion(f32[32,128]{1,0:T(8,128)S(1)} %fusion.10, s32[3200]{0:T(1024)S(1)} %reshape.50), kind=kCustom, calls=%fused_computation | custom fusion | bytes 51200 | tf_op jit(solution)/shard_map/jit(take_along_axis)/gather | solution.py:83
  649.0 0.1 reshape.53
  649.1 0.6 and_select_fusion
  (6 shorter events, 0.1 us)
Async XLA Ops:
  6.5 338.8 %copy-start = (s32[4096,100]{0,1:T(8,128)S(1)}, s32[4096,100]{0,1:T(8,128)}, u32[]{:S(2)}) copy-start(s32[4096,100]{0,1:T(8,128)} %param.19) | copy-start | bytes 4915204
  6.5 300.0 %all-gather.4.cloned.1.call-start = ((), (), s32[]{:S(2)}) async-start(), calls=%async_computation.2 | async-start | bytes 14155776 | tf_op jit(solution)/shard_map/all_gather | solution.py:13
  9.3 309.7 %all-gather.6.cloned.1.call-start = ((), (), s32[]{:S(2)}) async-start(), calls=%async_computation.3 | async-start | bytes 7077888 | tf_op jit(solution)/shard_map/all_gather | solution.py:53
  10.1 433.1 %reduce-scatter.2.cloned.1.call-start = ((), (), s32[]{:S(2)}) async-start(), calls=%async_computation.4 | async-start | bytes 8912896 | tf_op jit(solution)/shard_map/reduce_scatter | solution.py:56
  301.4 5.1 copy-start.3
  345.3 99.3 %copy-start.1 = (f32[4096]{0:T(1024)S(1)}, f32[4096]{0:T(1024)}, u32[]{:S(2)}) copy-start(f32[4096]{0:T(1024)} %param.15) | copy-start | bytes 49156
  446.1 182.6 %copy-start.2 = (s32[128]{0:T(128)S(1)}, s32[128]{0:T(128)}, u32[]{:S(2)}) copy-start(s32[128]{0:T(128)} %param.18) | copy-start | bytes 1540
Sparse Core Ops, SparseCore 0:
  9.4 134.2 all-gather.3
  145.3 70.9 all-gather.5
  345.4 97.6 reduce-scatter.1
